TPU v7x, 32 devices: a whole 2x2x4 slice. The times are simulated.
32 devices in a mesh: row: 8 (over y, x, core), col: 4 (over z).
Axes of the slice: x: 2, y: 2, z: 4, core: 2. Of those that a mesh axis runs over, the one named last changes fastest.
Arguments:
- block_values: bfloat16 [8, 4, 64, 256, 256], P('row', 'col'), may hold values from -0.1875 to 0.1875
- block_rows: int32 [8, 4, 64], P('row', 'col'), may hold values from 0 to 63
- block_cols: int32 [8, 4, 64], P('row', 'col'), may hold values from 0 to 255
- live_count: int32 [8, 4], P('row', 'col'), may hold values from 16 to 64, as said below
- objective: float32 [262144], P('col'), may hold values from -6 to 6
- upper_bound: float32 [262144], P('col'), may hold values from 0.5 to 2
- demand: float32 [131072], P('row'), may hold values from -6 to 6
- primal_start: float32 [262144], P('col'), may hold values from 0 to 0.5
- dual_start: float32 [131072], P('row'), may hold values from 0 to 0.5
- restart_at: int32 [8], replicated, may hold values 0 or 1
Outputs:
- primal_final: float32 [262144], P('col')
- dual_final: float32 [131072], P('row')
Inputs may be any that keep to these rules, and one draw needn't show every extreme that they name: `live_count`: each device's count of used slots; some device uses all 64.
All inputs are finite; a program needn't handle non-finite values.
Results may differ from a plain program's by a relative error of at most 0.0018.
Values may be sent and summed in bfloat16 or wider, within the bound.
A program may use at most 64 MiB of HBM per device.

v0:
```python
import jax
import jax.numpy as jnp
from jax import lax
from jax.sharding import PartitionSpec as P

ITERS = 8
step_scale = 0.3
epsilon = 1e-06


def shards(
    block_values,
    block_rows,
    block_cols,
    live_count,
    objective,
    upper_bound,
    demand,
    primal_start,
    dual_start,
    restart_at,
):
    slot_values = block_values[0, 0]
    rows_index = block_rows[0, 0]
    cols_index = block_cols[0, 0]
    used_slots = live_count[0, 0]
    slots = slot_values.shape[0]
    block_size = slot_values.shape[1]
    row_blocks = demand.shape[0] // block_size
    col_blocks = objective.shape[0] // block_size
    row_count = lax.axis_size("row")
    col_count = lax.axis_size("col")
    row_rank = lax.axis_index("row")
    col_rank = lax.axis_index("col")
    total_cols = objective.shape[0] * col_count
    total_rows = demand.shape[0] * row_count
    share_len = objective.shape[0] // row_count
    dual_len = demand.shape[0] // col_count
    live_slot = jnp.arange(slots, dtype=jnp.int32) < used_slots
    row_onehot = (
        (rows_index[:, None] == jnp.arange(row_blocks, dtype=jnp.int32)[None, :])
        & live_slot[:, None]
    ).astype(jnp.float32)
    col_onehot = (
        (cols_index[:, None] == jnp.arange(col_blocks, dtype=jnp.int32)[None, :])
        & live_slot[:, None]
    ).astype(jnp.float32)
    x = primal_start
    y = dual_start
    anchor_x = x
    anchor_y = y
    sum_x = jnp.zeros_like(x)
    sum_y = jnp.zeros_like(y)
    taken = jnp.zeros((), jnp.float32)
    omega = jnp.ones((), jnp.float32)
    for k in range(ITERS):
        step_primal = step_scale / omega
        step_dual = step_scale * omega
        y_low = y.astype(jnp.bfloat16)
        dual_pieces = y_low.reshape(row_blocks, block_size)[rows_index]
        dual_products = jnp.einsum(
            "tij,ti->tj", slot_values, dual_pieces, preferred_element_type=jnp.float32
        )
        dual_image = lax.psum(
            jnp.einsum(
                "tc,tj->cj", col_onehot, dual_products, precision=lax.Precision.HIGHEST
            ).reshape(-1),
            "row",
        )
        x_next = jnp.minimum(
            jnp.maximum(x - step_primal * (objective - dual_image), 0.0), upper_bound
        )
        extrap_low = (2.0 * x_next - x).astype(jnp.bfloat16)
        pieces = extrap_low.reshape(col_blocks, block_size)[cols_index]
        products = jnp.einsum("tij,tj->ti", slot_values, pieces, preferred_element_type=jnp.float32)
        primal_image = lax.psum(
            jnp.einsum("tr,ti->ri", row_onehot, products, precision=lax.Precision.HIGHEST).reshape(
                -1
            ),
            "col",
        )
        y_next = jnp.maximum(y + step_dual * (demand - primal_image), 0.0)
        x = x_next
        y = y_next
        sum_x = sum_x + x
        sum_y = sum_y + y
        taken = taken + 1.0
        if k <= ITERS - 3:
            is_restart = restart_at[k] == 1
            mean_x = sum_x / taken
            mean_y = sum_y / taken
            gap_x = lax.dynamic_slice_in_dim(mean_x - anchor_x, row_rank * share_len, share_len)
            gap_y = lax.dynamic_slice_in_dim(mean_y - anchor_y, col_rank * dual_len, dual_len)
            square_x = lax.psum(jnp.sum(gap_x * gap_x), ("row", "col"))
            square_y = lax.psum(jnp.sum(gap_y * gap_y), ("row", "col"))
            drift_x = square_x / total_cols + epsilon
            drift_y = square_y / total_rows + epsilon
            omega_next = jnp.sqrt(omega) * (drift_x / drift_y) ** 0.25
            x = jnp.where(is_restart, mean_x, x)
            y = jnp.where(is_restart, mean_y, y)
            anchor_x = jnp.where(is_restart, mean_x, anchor_x)
            anchor_y = jnp.where(is_restart, mean_y, anchor_y)
            sum_x = jnp.where(is_restart, jnp.zeros_like(sum_x), sum_x)
            sum_y = jnp.where(is_restart, jnp.zeros_like(sum_y), sum_y)
            taken = jnp.where(is_restart, jnp.zeros_like(taken), taken)
            omega = jnp.where(is_restart, omega_next, omega)
    return (x, y)


def solution(mesh):
    placed = (
        P("row", "col", None, None, None),
        P("row", "col", None),
        P("row", "col", None),
        P("row", "col"),
        P("col"),
        P("col"),
        P("row"),
        P("col"),
        P("row"),
        P(),
    )
    return jax.shard_map(
        shards, mesh=mesh, in_specs=placed, out_specs=(P("col"), P("row")), check_vma=False
    )
```

profile of v0, /device:TPU:0, one launch (start us, length us, event | category | flops | bytes accessed | tf_op | source)
XLA Modules:
  0.0 848.5 jit_solution(4290460746907200810)
XLA Ops:
  8.5 0.8 convert_element_type.50
  10.1 4.6 fusion.30
  15.2 0.8 copy.44
  16.1 56.7 %all-reduce.23.cloned.1.call-done = f32[65536]{0:T(1024)} async-done(((f32[65536]{0:T(1024)}), f32[65536]{0:T(1024)}) %all-reduce.23.cloned.1.call-update) | async-done | bytes 262160 | tf_op jit(solution)/shard_map/psum | solution.py:64
  72.8 1.0 subtract_convert_fusion.7
  73.9 0.7 gather_fusion.1
  74.6 5.6 fusion.28
  81.3 33.8 %all-reduce.25.cloned.1.call-done = f32[16384]{0:T(1024)} async-done(((f32[16384]{0:T(1024)}), f32[16384]{0:T(1024)}) %all-reduce.25.cloned.1.call-update) | async-done | bytes 65552 | tf_op jit(solution)/shard_map/psum | solution.py:76
  115.1 0.9 fusion.158
  116.7 4.6 fusion.26
  121.7 0.8 copy.46
  125.9 40.4 %all-reduce.5 = (f32[]{:T(128)}, f32[]{:T(128)}) all-reduce(f32[]{:T(128)} %fusion.98, f32[]{:T(128)} %fusion.138), channel_id=1, replica_groups=mesh['row'=8,'col'=4] {'row','col'}, use_global_device_ids=true, to_apply=%region_2.0 | all-reduce | flops 2 | bytes 16 | tf_op jit(solution)/shard_map/psum | solution.py:94
  167.7 8.6 %all-reduce.27.cloned.1.call-done = f32[65536]{0:T(1024)} async-done(((f32[65536]{0:T(1024)}), f32[65536]{0:T(1024)}) %all-reduce.27.cloned.1.call-update) | async-done | bytes 262160 | tf_op jit(solution)/shard_map/psum | solution.py:64
  176.3 1.0 broadcast_select_fusion.1
  178.1 5.6 fusion.24
  184.8 33.8 %all-reduce.29.cloned.1.call-done = f32[16384]{0:T(1024)} async-done(((f32[16384]{0:T(1024)}), f32[16384]{0:T(1024)}) %all-reduce.29.cloned.1.call-update) | async-done | bytes 65552 | tf_op jit(solution)/shard_map/psum | solution.py:76
  218.6 0.9 broadcast_select_fusion.15
  220.2 4.6 fusion.22
  225.2 0.8 copy.48
  227.5 40.3 %all-reduce.4 = (f32[]{:T(128)}, f32[]{:T(128)}) all-reduce(f32[]{:T(128)} %fusion.96, f32[]{:T(128)} %fusion.136), channel_id=1, replica_groups=mesh['row'=8,'col'=4] {'row','col'}, use_global_device_ids=true, to_apply=%region_8.9 | all-reduce | flops 2 | bytes 16 | tf_op jit(solution)/shard_map/psum | solution.py:94
  269.3 10.5 %all-reduce.31.cloned.1.call-done = f32[65536]{0:T(1024)} async-done(((f32[65536]{0:T(1024)}), f32[65536]{0:T(1024)}) %all-reduce.31.cloned.1.call-update) | async-done | bytes 262160 | tf_op jit(solution)/shard_map/psum | solution.py:64
  279.8 1.0 broadcast_divide_fusion.2
  281.7 5.6 fusion.20
  289.3 32.9 %all-reduce.33.cloned.1.call-done = f32[16384]{0:T(1024)} async-done(((f32[16384]{0:T(1024)}), f32[16384]{0:T(1024)}) %all-reduce.33.cloned.1.call-update) | async-done | bytes 65552 | tf_op jit(solution)/shard_map/psum | solution.py:76
  322.2 0.9 fusion.125
  323.8 4.6 fusion.18
  328.8 0.8 copy.50
  331.5 40.3 %all-reduce.3 = (f32[]{:T(128)}, f32[]{:T(128)}) all-reduce(f32[]{:T(128)} %fusion.94, f32[]{:T(128)} %fusion.134), channel_id=1, replica_groups=mesh['row'=8,'col'=4] {'row','col'}, use_global_device_ids=true, to_apply=%region_14.15 | all-reduce | flops 2 | bytes 16 | tf_op jit(solution)/shard_map/psum | solution.py:94
  373.1 10.3 %all-reduce.35.cloned.1.call-done = f32[65536]{0:T(1024)} async-done(((f32[65536]{0:T(1024)}), f32[65536]{0:T(1024)}) %all-reduce.35.cloned.1.call-update) | async-done | bytes 262160 | tf_op jit(solution)/shard_map/psum | solution.py:64
  383.4 1.1 broadcast_select_fusion.5
  385.2 5.6 fusion.16
  391.9 33.8 %all-reduce.37.cloned.1.call-done = f32[16384]{0:T(1024)} async-done(((f32[16384]{0:T(1024)}), f32[16384]{0:T(1024)}) %all-reduce.37.cloned.1.call-update) | async-done | bytes 65552 | tf_op jit(solution)/shard_map/psum | solution.py:76
  425.7 0.9 broadcast_select_fusion.11
  427.4 4.6 fusion.14
  432.3 0.8 copy.52
  434.5 40.3 %all-reduce.2 = (f32[]{:T(128)}, f32[]{:T(128)}) all-reduce(f32[]{:T(128)} %fusion.92, f32[]{:T(128)} %fusion.132), channel_id=1, replica_groups=mesh['row'=8,'col'=4] {'row','col'}, use_global_device_ids=true, to_apply=%region_20.21 | all-reduce | flops 2 | bytes 16 | tf_op jit(solution)/shard_map/psum | solution.py:94
  476.1 10.8 %all-reduce.39.cloned.1.call-done = f32[65536]{0:T(1024)} async-done(((f32[65536]{0:T(1024)}), f32[65536]{0:T(1024)}) %all-reduce.39.cloned.1.call-update) | async-done | bytes 262160 | tf_op jit(solution)/shard_map/psum | solution.py:64
  487.0 1.0 broadcast_divide_fusion
  488.8 5.6 fusion.12
  496.2 33.2 %all-reduce.41.cloned.1.call-done = f32[16384]{0:T(1024)} async-done(((f32[16384]{0:T(1024)}), f32[16384]{0:T(1024)}) %all-reduce.41.cloned.1.call-update) | async-done | bytes 65552 | tf_op jit(solution)/shard_map/psum | solution.py:76
  529.3 0.9 fusion.127
  530.9 4.6 fusion.10
  535.9 0.8 copy.54
  538.1 40.3 %all-reduce.1 = (f32[]{:T(128)}, f32[]{:T(128)}) all-reduce(f32[]{:T(128)} %multiply_reduce_fusion, f32[]{:T(128)} %multiply_reduce_fusion.1), channel_id=1, replica_groups=mesh['row'=8,'col'=4] {'row','col'}, use_global_device_ids=true, to_apply=%region_26.27 | all-reduce | flops 2 | bytes 16 | tf_op jit(solution)/shard_map/psum | solution.py:94
  579.9 10.7 %all-reduce.43.cloned.1.call-done = f32[65536]{0:T(1024)} async-done(((f32[65536]{0:T(1024)}), f32[65536]{0:T(1024)}) %all-reduce.43.cloned.1.call-update) | async-done | bytes 262160 | tf_op jit(solution)/shard_map/psum | solution.py:64
  590.6 1.0 add_divide_fusion
  592.4 5.6 fusion.8
  600.0 33.0 %all-reduce.45.cloned.1.call-done = f32[16384]{0:T(1024)} async-done(((f32[16384]{0:T(1024)}), f32[16384]{0:T(1024)}) %all-reduce.45.cloned.1.call-update) | async-done | bytes 65552 | tf_op jit(solution)/shard_map/psum | solution.py:76
  632.9 0.9 fusion.128
  634.5 4.6 fusion.6
  639.5 0.8 copy.56
  641.7 40.4 %all-reduce = (f32[]{:T(128)}, f32[]{:T(128)}) all-reduce(f32[]{:T(128)} %fusion.90, f32[]{:T(128)} %fusion.130), channel_id=1, replica_groups=mesh['row'=8,'col'=4] {'row','col'}, use_global_device_ids=true, to_apply=%region_32.33 | all-reduce | flops 2 | bytes 16 | tf_op jit(solution)/shard_map/psum | solution.py:94
  683.5 10.6 %all-reduce.47.cloned.1.call-done = f32[65536]{0:T(1024)} async-done(((f32[65536]{0:T(1024)}), f32[65536]{0:T(1024)}) %all-reduce.47.cloned.1.call-update) | async-done | bytes 262160 | tf_op jit(solution)/shard_map/psum | solution.py:64
  694.1 1.0 subtract_convert_fusion.1
  695.9 5.6 fusion.4
  702.6 33.8 %all-reduce.49.cloned.1.call-done = f32[16384]{0:T(1024)} async-done(((f32[16384]{0:T(1024)}), f32[16384]{0:T(1024)}) %all-reduce.49.cloned.1.call-update) | async-done | bytes 65552 | tf_op jit(solution)/shard_map/psum | solution.py:76
  736.4 0.9 fusion.157
  738.0 4.6 fusion.2
  743.0 0.8 copy.58
  743.9 53.7 %all-reduce.51.cloned.1.call-done = f32[65536]{0:T(1024)} async-done(((f32[65536]{0:T(1024)}), f32[65536]{0:T(1024)}) %all-reduce.51.cloned.1.call-update) | async-done | bytes 262160 | tf_op jit(solution)/shard_map/psum | solution.py:64
  797.6 1.7 subtract_convert_fusion
  800.0 5.6 fusion
  806.7 33.8 %all-reduce.53.cloned.1.call-done = f32[16384]{0:T(1024)} async-done(((f32[16384]{0:T(1024)}), f32[16384]{0:T(1024)}) %all-reduce.53.cloned.1.call-update) | async-done | bytes 65552 | tf_op jit(solution)/shard_map/psum | solution.py:76
  840.5 1.5 add_maximum_fusion
  (128 shorter events, 32.5 us)
Async XLA Ops:
  7.2 7.6 copy-start.5
  7.2 65.6 %all-reduce.23.cloned.1.call-start = ((), (), s32[]{:S(2)}) async-start(), calls=%async_computation | async-start | bytes 524288 | tf_op jit(solution)/shard_map/psum | solution.py:64
  10.1 62.7 %copy-start = (f32[65536]{0:T(1024)S(1)}, f32[65536]{0:T(1024)}, u32[]{:S(2)}) copy-start(f32[65536]{0:T(1024)} %param.15) | copy-start | bytes 786436
  10.1 62.7 %copy-start.1 = (f32[65536]{0:T(1024)S(1)}, f32[65536]{0:T(1024)}, u32[]{:S(2)}) copy-start(f32[65536]{0:T(1024)} %param.14) | copy-start | bytes 786436
  10.1 62.7 %copy-start.3 = (f32[65536]{0:T(1024)S(1)}, f32[65536]{0:T(1024)}, u32[]{:S(2)}) copy-start(f32[65536]{0:T(1024)} %param.17) | copy-start | bytes 786436
  14.8 65.4 %copy-start.6 = (s32[1,1,64]{2,1,0:T(1,128)S(1)}, s32[1,1,64]{2,1,0:T(1,128)}, u32[]{:S(2)}) copy-start(s32[1,1,64]{2,1,0:T(1,128)} %param.11) | copy-start | bytes 772
  14.8 100.3 %copy-start.2 = (f32[16384]{0:T(1024)S(1)}, f32[16384]{0:T(1024)}, u32[]{:S(2)}) copy-start(f32[16384]{0:T(1024)} %param.16) | copy-start | bytes 196612
  14.8 100.3 %copy-start.4 = (f32[16384]{0:T(1024)S(1)}, f32[16384]{0:T(1024)}, u32[]{:S(2)}) copy-start(f32[16384]{0:T(1024)} %param.18) | copy-start | bytes 196612
  16.1 99.0 %all-reduce.25.cloned.1.call-start = ((), (), s32[]{:S(2)}) async-start(), calls=%async_computation.1 | async-start | bytes 131072 | tf_op jit(solution)/shard_map/psum | solution.py:76
  81.2 95.0 %all-reduce.27.cloned.1.call-start = ((), (), s32[]{:S(2)}) async-start(), calls=%async_computation.2 | async-start | bytes 524288 | tf_op jit(solution)/shard_map/psum | solution.py:64
  116.7 5.9 copy-start.7
  122.5 96.1 %all-reduce.29.cloned.1.call-start = ((), (), s32[]{:S(2)}) async-start(), calls=%async_computation.3 | async-start | bytes 131072 | tf_op jit(solution)/shard_map/psum | solution.py:76
  184.8 95.1 %all-reduce.31.cloned.1.call-start = ((), (), s32[]{:S(2)}) async-start(), calls=%async_computation.4 | async-start | bytes 524288 | tf_op jit(solution)/shard_map/psum | solution.py:64
  226.1 96.1 %all-reduce.33.cloned.1.call-start = ((), (), s32[]{:S(2)}) async-start(), calls=%async_computation.5 | async-start | bytes 131072 | tf_op jit(solution)/shard_map/psum | solution.py:76
  288.3 95.1 %all-reduce.35.cloned.1.call-start = ((), (), s32[]{:S(2)}) async-start(), calls=%async_computation.6 | async-start | bytes 524288 | tf_op jit(solution)/shard_map/psum | solution.py:64
  329.6 96.1 %all-reduce.37.cloned.1.call-start = ((), (), s32[]{:S(2)}) async-start(), calls=%async_computation.7 | async-start | bytes 131072 | tf_op jit(solution)/shard_map/psum | solution.py:76
  391.9 95.1 %all-reduce.39.cloned.1.call-start = ((), (), s32[]{:S(2)}) async-start(), calls=%async_computation.8 | async-start | bytes 524288 | tf_op jit(solution)/shard_map/psum | solution.py:64
  433.2 96.1 %all-reduce.41.cloned.1.call-start = ((), (), s32[]{:S(2)}) async-start(), calls=%async_computation.9 | async-start | bytes 131072 | tf_op jit(solution)/shard_map/psum | solution.py:76
  495.5 95.1 %all-reduce.43.cloned.1.call-start = ((), (), s32[]{:S(2)}) async-start(), calls=%async_computation.10 | async-start | bytes 524288 | tf_op jit(solution)/shard_map/psum | solution.py:64
  536.8 96.1 %all-reduce.45.cloned.1.call-start = ((), (), s32[]{:S(2)}) async-start(), calls=%async_computation.11 | async-start | bytes 131072 | tf_op jit(solution)/shard_map/psum | solution.py:76
  599.1 95.0 %all-reduce.47.cloned.1.call-start = ((), (), s32[]{:S(2)}) async-start(), calls=%async_computation.12 | async-start | bytes 524288 | tf_op jit(solution)/shard_map/psum | solution.py:64
  640.4 96.0 %all-reduce.49.cloned.1.call-start = ((), (), s32[]{:S(2)}) async-start(), calls=%async_computation.13 | async-start | bytes 131072 | tf_op jit(solution)/shard_map/psum | solution.py:76
  702.5 95.0 %all-reduce.51.cloned.1.call-start = ((), (), s32[]{:S(2)}) async-start(), calls=%async_computation.14 | async-start | bytes 524288 | tf_op jit(solution)/shard_map/psum | solution.py:64
  743.8 96.7 %all-reduce.53.cloned.1.call-start = ((), (), s32[]{:S(2)}) async-start(), calls=%async_computation.15 | async-start | bytes 131072 | tf_op jit(solution)/shard_map/psum | solution.py:76
Sparse Core Ops, SparseCore 0:
  16.2 56.5 all-reduce.22
  81.4 33.6 all-reduce.24
  122.7 53.5 all-reduce.26
  184.9 33.6 all-reduce.28
  226.2 53.5 all-reduce.30
  288.5 33.7 all-reduce.32
  329.8 53.5 all-reduce.34
  392.0 33.6 all-reduce.36
  433.3 53.6 all-reduce.38
  495.6 33.6 all-reduce.40
  536.9 53.6 all-reduce.42
  599.2 33.6 all-reduce.44
  640.5 53.5 all-reduce.46
  702.7 33.6 all-reduce.48
  743.9 53.5 all-reduce.50
  806.8 33.6 all-reduce.52
where the time goes:
time: 850 us; the launch traced here: 849 us
  waiting for transfers between devices  440 us (52%)
  blocking collectives  242 us (28%)
  matrix products  87.5 us (10%)
  between operations  27.6 us (3%)
  other arithmetic  25.7 us (3%)
  local copies, waits for them, and re-layouts  24.5 us (3%)
    psum x8, waiting for transfers between devices, shards(): lax.psum(jnp.einsum('tr,ti->ri', row_onehot, products, precision=lax.Prec...  268 us
    psum x6, blocking collectives, shards(): square_x = lax.psum(jnp.sum(gap_x * gap_x), ('row', 'col'))  242 us
    psum x8, waiting for transfers between devices, shards(): lax.psum(jnp.einsum('tc,tj->cj', col_onehot, dual_products, precision=lax...  172 us
    dot_general x8, matrix products, shards(): jnp.einsum('tij,tj->ti', slot_values, pieces, preferred_element_type=jnp....  45.1 us
    dot_general x8, matrix products, shards(): jnp.einsum('tij,ti->tj', slot_values, dual_pieces, preferred_element_type...  36.7 us
  transfers between devices with their start and end apart: 16, of which 16 were waited for; matrix products, arithmetic and copies ran while one was open for 1% of the time, Pallas kernels for 0%

commit v1 on v0

--- a/solution.py
+++ b/solution.py
@@ -61,11 +61,11 @@
         dual_products = jnp.einsum(
             "tij,ti->tj", slot_values, dual_pieces, preferred_element_type=jnp.float32
         )
-        dual_image = lax.psum(
+        _recover_space = lambda buf: jnp.sum(lax.all_gather(buf, "row"), axis=0)
+        dual_image = _recover_space(
             jnp.einsum(
                 "tc,tj->cj", col_onehot, dual_products, precision=lax.Precision.HIGHEST
-            ).reshape(-1),
-            "row",
+            ).reshape(-1)
         )
         x_next = jnp.minimum(
             jnp.maximum(x - step_primal * (objective - dual_image), 0.0), upper_bound

time: 850 us -> 767 us (0.902)
  waiting for transfers between devices: 440 us -> 330 us
  other arithmetic: 25.7 us -> 43.1 us
    psum x8 -> x0, waiting for transfers between devices: 172 us -> none  [shards(): lax.psum(jnp.einsum('tc,tj->cj', col_onehot, dual_products, precision=lax...]
    all_gather x0 -> x8, waiting for transfers between devices: none -> 58.3 us  [shards(): _recover_space = lambda buf: jnp.sum(lax.all_gather(buf, 'row'), axis=0)]
    reduce_sum x0 -> x8, other arithmetic: none -> 25 us  [shards(): _recover_space = lambda buf: jnp.sum(lax.all_gather(buf, 'row'), axis=0)]
  transfers between devices with their start and end apart: 16 -> 16, of which waited for: 16 -> 10; matrix products, arithmetic and copies ran while one was open for 1% -> 1% of each run, Pallas kernels for 0% -> 0%
where the time goes in v1:
time: 767 us; the launch traced here: 758 us
  waiting for transfers between devices  330 us (43%)
  blocking collectives  242 us (32%)
  matrix products  87.5 us (11%)
  other arithmetic  43.1 us (6%)
  between operations  27.8 us (4%)
  local copies, waits for them, and re-layouts  25.5 us (3%)
    psum x8, waiting for transfers between devices, shards(): lax.psum(jnp.einsum('tr,ti->ri', row_onehot, products, precision=lax.Prec...  272 us
    psum x6, blocking collectives, shards(): square_x = lax.psum(jnp.sum(gap_x * gap_x), ('row', 'col'))  242 us
    all_gather x8, waiting for transfers between devices, shards(): _recover_space = lambda buf: jnp.sum(lax.all_gather(buf, 'row'), axis=0)  58.3 us
    dot_general x8, matrix products, shards(): jnp.einsum('tij,tj->ti', slot_values, pieces, preferred_element_type=jnp....  45.1 us
    dot_general x8, matrix products, shards(): jnp.einsum('tij,ti->tj', slot_values, dual_pieces, preferred_element_type...  36.7 us
    reduce_sum x8, other arithmetic, shards(): _recover_space = lambda buf: jnp.sum(lax.all_gather(buf, 'row'), axis=0)  25 us
  transfers between devices with their start and end apart: 16, of which 10 were waited for; matrix products, arithmetic and copies ran while one was open for 1% of the time, Pallas kernels for 0%

profile of v1, /device:TPU:0, one launch (start us, length us, event | category | flops | bytes accessed | tf_op | source)
XLA Modules:
  0.0 757.6 jit_solution(10503436677816793574)
XLA Ops:
  8.5 0.8 convert_element_type.50
  9.4 0.7 gather_fusion
  10.1 4.6 fusion.30
  15.2 1.0 reshape.302
  16.3 30.6 %all-gather.17.cloned.1.call-done = f32[8,1,65536]{2,1,0:T(1,128)} async-done(((f32[1,1,65536]{2,1,0:T(1,128)}), f32[8,1,65536]{2,1,0:T(1,128)}) %all-gather.17.cloned.1.call-update) | async-done | bytes 2097168 | tf_op jit(solution)/shard_map/all_gather | solution.py:64
  46.9 3.1 reduce_sum.180
  50.1 0.7 gather_fusion.1
  50.8 5.6 fusion.28
  57.5 34.4 %all-reduce.15.cloned.1.call-done = f32[16384]{0:T(1024)} async-done(((f32[16384]{0:T(1024)}), f32[16384]{0:T(1024)}) %all-reduce.15.cloned.1.call-update) | async-done | bytes 65552 | tf_op jit(solution)/shard_map/psum | solution.py:76
  92.0 0.9 fusion.166
  92.8 0.7 gather_fusion.2
  93.6 4.6 fusion.26
  98.5 1.0 reshape.304
  102.7 40.3 %all-reduce.5 = (f32[]{:T(128)}, f32[]{:T(128)}) all-reduce(f32[]{:T(128)} %fusion.106, f32[]{:T(128)} %fusion.146), channel_id=1, replica_groups=mesh['row'=8,'col'=4] {'row','col'}, use_global_device_ids=true, to_apply=%region_2.0 | all-reduce | flops 2 | bytes 16 | tf_op jit(solution)/shard_map/psum | solution.py:94
  144.6 3.1 reduce_sum.183
  147.9 0.7 gather_fusion.3
  148.6 5.6 fusion.24
  155.8 33.8 %all-reduce.17.cloned.1.call-done = f32[16384]{0:T(1024)} async-done(((f32[16384]{0:T(1024)}), f32[16384]{0:T(1024)}) %all-reduce.17.cloned.1.call-update) | async-done | bytes 65552 | tf_op jit(solution)/shard_map/psum | solution.py:76
  189.5 0.9 broadcast_select_fusion.15
  190.5 0.7 gather_fusion.4
  191.2 4.6 fusion.22
  196.1 1.0 reshape.306
  198.4 40.3 %all-reduce.4 = (f32[]{:T(128)}, f32[]{:T(128)}) all-reduce(f32[]{:T(128)} %fusion.104, f32[]{:T(128)} %fusion.144), channel_id=1, replica_groups=mesh['row'=8,'col'=4] {'row','col'}, use_global_device_ids=true, to_apply=%region_8.9 | all-reduce | flops 2 | bytes 16 | tf_op jit(solution)/shard_map/psum | solution.py:94
  240.1 3.1 reduce_sum.186
  243.4 0.7 gather_fusion.5
  244.1 5.6 fusion.20
  251.5 33.7 %all-reduce.19.cloned.1.call-done = f32[16384]{0:T(1024)} async-done(((f32[16384]{0:T(1024)}), f32[16384]{0:T(1024)}) %all-reduce.19.cloned.1.call-update) | async-done | bytes 65552 | tf_op jit(solution)/shard_map/psum | solution.py:76
  285.1 0.9 fusion.133
  286.7 4.6 fusion.18
  291.7 1.0 reshape.308
  294.7 40.5 %all-reduce.3 = (f32[]{:T(128)}, f32[]{:T(128)}) all-reduce(f32[]{:T(128)} %fusion.102, f32[]{:T(128)} %fusion.142), channel_id=1, replica_groups=mesh['row'=8,'col'=4] {'row','col'}, use_global_device_ids=true, to_apply=%region_14.15 | all-reduce | flops 2 | bytes 16 | tf_op jit(solution)/shard_map/psum | solution.py:94
  336.6 3.1 reduce_sum.189
  340.6 5.6 fusion.16
  347.5 33.9 %all-reduce.21.cloned.1.call-done = f32[16384]{0:T(1024)} async-done(((f32[16384]{0:T(1024)}), f32[16384]{0:T(1024)}) %all-reduce.21.cloned.1.call-update) | async-done | bytes 65552 | tf_op jit(solution)/shard_map/psum | solution.py:76
  381.4 0.9 broadcast_select_fusion.11
  383.0 4.6 fusion.14
  388.0 1.0 reshape.310
  390.3 40.3 %all-reduce.2 = (f32[]{:T(128)}, f32[]{:T(128)}) all-reduce(f32[]{:T(128)} %fusion.100, f32[]{:T(128)} %fusion.140), channel_id=1, replica_groups=mesh['row'=8,'col'=4] {'row','col'}, use_global_device_ids=true, to_apply=%region_20.21 | all-reduce | flops 2 | bytes 16 | tf_op jit(solution)/shard_map/psum | solution.py:94
  432.1 3.1 reduce_sum.192
  436.1 5.6 fusion.12
  443.4 33.7 %all-reduce.23.cloned.1.call-done = f32[16384]{0:T(1024)} async-done(((f32[16384]{0:T(1024)}), f32[16384]{0:T(1024)}) %all-reduce.23.cloned.1.call-update) | async-done | bytes 65552 | tf_op jit(solution)/shard_map/psum | solution.py:76
  477.1 0.9 fusion.135
  478.7 4.6 fusion.10
  483.7 1.0 reshape.312
  486.0 40.3 %all-reduce.1 = (f32[]{:T(128)}, f32[]{:T(128)}) all-reduce(f32[]{:T(128)} %multiply_reduce_fusion, f32[]{:T(128)} %multiply_reduce_fusion.1), channel_id=1, replica_groups=mesh['row'=8,'col'=4] {'row','col'}, use_global_device_ids=true, to_apply=%region_26.27 | all-reduce | flops 2 | bytes 16 | tf_op jit(solution)/shard_map/psum | solution.py:94
  527.8 3.1 reduce_sum.195
  531.8 5.6 fusion.8
  539.3 33.5 %all-reduce.25.cloned.1.call-done = f32[16384]{0:T(1024)} async-done(((f32[16384]{0:T(1024)}), f32[16384]{0:T(1024)}) %all-reduce.25.cloned.1.call-update) | async-done | bytes 65552 | tf_op jit(solution)/shard_map/psum | solution.py:76
  572.8 0.9 fusion.136
  574.4 4.6 fusion.6
  579.4 1.0 reshape.314
  581.7 40.3 %all-reduce = (f32[]{:T(128)}, f32[]{:T(128)}) all-reduce(f32[]{:T(128)} %fusion.98, f32[]{:T(128)} %fusion.138), channel_id=1, replica_groups=mesh['row'=8,'col'=4] {'row','col'}, use_global_device_ids=true, to_apply=%region_32.33 | all-reduce | flops 2 | bytes 16 | tf_op jit(solution)/shard_map/psum | solution.py:94
  623.5 3.1 reduce_sum.198
  627.4 5.6 fusion.4
  634.1 34.3 %all-reduce.27.cloned.1.call-done = f32[16384]{0:T(1024)} async-done(((f32[16384]{0:T(1024)}), f32[16384]{0:T(1024)}) %all-reduce.27.cloned.1.call-update) | async-done | bytes 65552 | tf_op jit(solution)/shard_map/psum | solution.py:76
  668.4 0.9 fusion.165
  670.0 4.6 fusion.2
  675.0 1.0 reshape.316
  676.0 27.6 %all-gather.31.cloned.1.call-done = f32[8,1,65536]{2,1,0:T(1,128)} async-done(((f32[1,1,65536]{2,1,0:T(1,128)}), f32[8,1,65536]{2,1,0:T(1,128)}) %all-gather.31.cloned.1.call-update) | async-done | bytes 2097168 | tf_op jit(solution)/shard_map/all_gather | solution.py:64
  703.6 3.1 reduce_sum.199
  706.7 0.8 subtract_convert_fusion
  708.3 5.6 fusion
  714.9 34.5 %all-reduce.29.cloned.1.call-done = f32[16384]{0:T(1024)} async-done(((f32[16384]{0:T(1024)}), f32[16384]{0:T(1024)}) %all-reduce.29.cloned.1.call-update) | async-done | bytes 65552 | tf_op jit(solution)/shard_map/psum | solution.py:76
  749.4 1.5 add_maximum_fusion
  (136 shorter events, 30.1 us)
Async XLA Ops:
  7.2 7.6 %copy-start.5 = (s32[1,1,64]{2,1,0:T(1,128)S(1)}, s32[1,1,64]{2,1,0:T(1,128)}, u32[]{:S(2)}) copy-start(s32[1,1,64]{2,1,0:T(1,128)} %param.12) | copy-start | bytes 772
  7.2 39.7 %all-gather.17.cloned.1.call-start = ((), (), s32[]{:S(2)}) async-start(), calls=%async_computation.8 | async-start | bytes 2359296 | tf_op jit(solution)/shard_map/all_gather | solution.py:64
  10.1 39.9 %copy-start = (f32[65536]{0:T(1024)S(1)}, f32[65536]{0:T(1024)}, u32[]{:S(2)}) copy-start(f32[65536]{0:T(1024)} %param.15) | copy-start | bytes 786436
  10.1 39.9 %copy-start.1 = (f32[65536]{0:T(1024)S(1)}, f32[65536]{0:T(1024)}, u32[]{:S(2)}) copy-start(f32[65536]{0:T(1024)} %param.14) | copy-start | bytes 786436
  10.1 39.9 %copy-start.3 = (f32[65536]{0:T(1024)S(1)}, f32[65536]{0:T(1024)}, u32[]{:S(2)}) copy-start(f32[65536]{0:T(1024)} %param.17) | copy-start | bytes 786436
  14.8 41.7 %copy-start.6 = (s32[1,1,64]{2,1,0:T(1,128)S(1)}, s32[1,1,64]{2,1,0:T(1,128)}, u32[]{:S(2)}) copy-start(s32[1,1,64]{2,1,0:T(1,128)} %param.11) | copy-start | bytes 772
  14.8 77.2 %copy-start.2 = (f32[16384]{0:T(1024)S(1)}, f32[16384]{0:T(1024)}, u32[]{:S(2)}) copy-start(f32[16384]{0:T(1024)} %param.16) | copy-start | bytes 196612
  14.8 77.2 %copy-start.4 = (f32[16384]{0:T(1024)S(1)}, f32[16384]{0:T(1024)}, u32[]{:S(2)}) copy-start(f32[16384]{0:T(1024)} %param.18) | copy-start | bytes 196612
  16.2 75.8 %all-reduce.15.cloned.1.call-start = ((), (), s32[]{:S(2)}) async-start(), calls=%async_computation | async-start | bytes 131072 | tf_op jit(solution)/shard_map/psum | solution.py:76
  57.5 87.1 %all-gather.19.cloned.1.call-start = ((), (), s32[]{:S(2)}) async-start(), calls=%async_computation.9 | async-start | bytes 2359296 | tf_op jit(solution)/shard_map/all_gather | solution.py:64
  93.5 6.0 copy-start.7
  99.5 90.0 %all-reduce.17.cloned.1.call-start = ((), (), s32[]{:S(2)}) async-start(), calls=%async_computation.1 | async-start | bytes 131072 | tf_op jit(solution)/shard_map/psum | solution.py:76
  155.2 84.9 %all-gather.21.cloned.1.call-start = ((), (), s32[]{:S(2)}) async-start(), calls=%async_computation.10 | async-start | bytes 2359296 | tf_op jit(solution)/shard_map/all_gather | solution.py:64
  197.1 88.0 %all-reduce.19.cloned.1.call-start = ((), (), s32[]{:S(2)}) async-start(), calls=%async_computation.2 | async-start | bytes 131072 | tf_op jit(solution)/shard_map/psum | solution.py:76
  250.8 85.8 %all-gather.23.cloned.1.call-start = ((), (), s32[]{:S(2)}) async-start(), calls=%async_computation.11 | async-start | bytes 2359296 | tf_op jit(solution)/shard_map/all_gather | solution.py:64
  292.7 88.7 %all-reduce.21.cloned.1.call-start = ((), (), s32[]{:S(2)}) async-start(), calls=%async_computation.3 | async-start | bytes 131072 | tf_op jit(solution)/shard_map/psum | solution.py:76
  347.2 84.8 %all-gather.25.cloned.1.call-start = ((), (), s32[]{:S(2)}) async-start(), calls=%async_computation.12 | async-start | bytes 2359296 | tf_op jit(solution)/shard_map/all_gather | solution.py:64
  389.0 88.1 %all-reduce.23.cloned.1.call-start = ((), (), s32[]{:S(2)}) async-start(), calls=%async_computation.4 | async-start | bytes 131072 | tf_op jit(solution)/shard_map/psum | solution.py:76
  442.8 85.0 %all-gather.27.cloned.1.call-start = ((), (), s32[]{:S(2)}) async-start(), calls=%async_computation.13 | async-start | bytes 2359296 | tf_op jit(solution)/shard_map/all_gather | solution.py:64
  484.7 88.1 %all-reduce.25.cloned.1.call-start = ((), (), s32[]{:S(2)}) async-start(), calls=%async_computation.5 | async-start | bytes 131072 | tf_op jit(solution)/shard_map/psum | solution.py:76
  538.5 85.0 %all-gather.29.cloned.1.call-start = ((), (), s32[]{:S(2)}) async-start(), calls=%async_computation.14 | async-start | bytes 2359296 | tf_op jit(solution)/shard_map/all_gather | solution.py:64
  580.4 88.0 %all-reduce.27.cloned.1.call-start = ((), (), s32[]{:S(2)}) async-start(), calls=%async_computation.6 | async-start | bytes 131072 | tf_op jit(solution)/shard_map/psum | solution.py:76
  634.1 69.5 %all-gather.31.cloned.1.call-start = ((), (), s32[]{:S(2)}) async-start(), calls=%async_computation.15 | async-start | bytes 2359296 | tf_op jit(solution)/shard_map/all_gather | solution.py:64
  676.0 73.4 %all-reduce.29.cloned.1.call-start = ((), (), s32[]{:S(2)}) async-start(), calls=%async_computation.7 | async-start | bytes 131072 | tf_op jit(solution)/shard_map/psum | solution.py:76
Sparse Core Ops, SparseCore 0:
  16.3 30.4 all-gather.16
  57.6 34.2 all-reduce.14
  99.7 27.6 all-gather.18
  155.4 34.1 all-reduce.16
  197.3 27.6 all-gather.20
  250.9 34.1 all-reduce.18
  292.8 27.6 all-gather.22
  347.4 33.9 all-reduce.20
  389.1 27.6 all-gather.24
  442.9 34.1 all-reduce.22
  484.8 27.6 all-gather.26
  538.6 34.1 all-reduce.24
  580.5 27.6 all-gather.28
  634.2 34.1 all-reduce.26
  676.1 27.4 all-gather.30
  715.0 34.2 all-reduce.28
